TPU v7x, 128 devices: a whole 4x4x4 slice. The times are simulated.
128 devices in a mesh: section: 4 (over x), dp: 8 (over z_lo, y), tensor: 4 (over z_hi, core).
Axes of the slice: x: 4, y: 4, z: 4 (z_hi: 2, z_lo: 2; z = z_hi * 2 + z_lo), core: 2. Of those that a mesh axis runs over, the one named last changes fastest.
Arguments:
- saved: bfloat16 [4, 4096, 5120], P('section', ('dp', 'tensor')), may hold values from -0.09375 to 0.09375
- weight: bfloat16 [4, 5120, 5120], P('section', None, 'tensor'), may hold values from -0.078125 to 0.078125
- out_grad: bfloat16 [4096, 5120], P(('dp', 'tensor')), may hold values from -6 to 6
Outputs:
- input_grads: bfloat16 [4, 4096, 5120], P('section', ('dp', 'tensor'))
- weight_grads: float32 [4, 5120, 5120], P('section', 'dp', 'tensor')
All inputs are finite; a program needn't handle non-finite values.
Results may differ from a plain program's by a relative error of at most 0.02.
Values may be sent and summed in bfloat16 or wider, within the bound.
A program may use at most 192 MiB of HBM per device.

v0:
```python
import jax
import jax.numpy as jnp
from jax import lax
from jax.sharding import PartitionSpec as P


def from_behind(block, axis, distance):
    devices = range(lax.axis_size(axis))
    route = [(i - distance, i) for i in devices if i - distance in devices]
    return lax.ppermute(block, axis, route)


def on_device(saved, weight, out_grad):
    activations = saved[0]
    weight_cols = weight[0]
    sections = lax.axis_size("section")
    section_index = lax.axis_index("section")
    gradient = out_grad
    own_input = jnp.zeros(out_grad.shape, jnp.bfloat16)
    kept_columns = jnp.zeros(
        (out_grad.shape[0] * lax.axis_size("tensor"), weight_cols.shape[1]), jnp.bfloat16
    )
    for rounds in range(sections):
        active = sections - 1 - rounds
        on_duty = section_index == active
        columns = lax.all_to_all(gradient, "tensor", split_axis=1, concat_axis=0, tiled=True)

        def compute(operand):
            return lax.dot_general(
                operand, weight_cols, (((1,), (1,)), ((), ())), preferred_element_type=jnp.float32
            )

        def nothing(operand):
            return jnp.zeros((operand.shape[0], weight_cols.shape[0]), jnp.float32)

        returned = lax.psum_scatter(
            lax.cond(on_duty, compute, nothing, columns).astype(jnp.bfloat16),
            "tensor",
            scatter_dimension=0,
            tiled=True,
        ).astype(jnp.float32)
        updated = (gradient.astype(jnp.float32) + returned).astype(jnp.bfloat16)
        own_input = jnp.where(on_duty, updated, own_input)
        kept_columns = jnp.where(on_duty, columns, kept_columns)
        if rounds + 1 < sections:
            gradient = from_behind(updated, "section", -1)
    gathered = lax.all_gather(activations, "tensor", axis=0, tiled=True)
    weight_grad = lax.psum_scatter(
        lax.dot_general(
            gathered, kept_columns, (((0,), (0,)), ((), ())), preferred_element_type=jnp.float32
        ).astype(jnp.bfloat16),
        "dp",
        scatter_dimension=0,
        tiled=True,
    ).astype(jnp.float32)
    return (own_input[None], weight_grad[None])


def solution(mesh):
    placed = (
        P("section", ("dp", "tensor"), None),
        P("section", None, "tensor"),
        P(("dp", "tensor"), None),
    )
    return jax.shard_map(
        on_device,
        mesh=mesh,
        in_specs=placed,
        out_specs=(P("section", ("dp", "tensor"), None), P("section", "dp", "tensor")),
        check_vma=False,
    )
```

profile of v0, /device:TPU:1, one launch (start us, length us, event | category | flops | bytes accessed | tf_op | source)
XLA Modules:
  0.0 710.5 jit_solution(3716013409856002741)
XLA Ops:
  7.2 2.5 copy.46
  9.6 6.6 all-to-all-start
  16.3 17.9 %all-to-all-done = bf16[128,4,1280]{2,0,1:T(8,128)(2,1)S(1)} async-done(((bf16[128,4,1280]{2,0,1:T(8,128)(2,1)}), bf16[128,4,1280]{2,0,1:T(8,128)(2,1)S(1)}, u32[]{:S(2)}, u32[]{:S(2)}) %all-to-all-start) | async-done | bytes 1310752 | tf_op jit(solution)/shard_map/all_to_all | solution.py:26
  34.2 1.1 copy-done.4
  35.2 3.0 conditional.4
  35.2 3.0 broadcast.8
  38.2 7.9 %copy.25 = bf16[512,5120]{0,1:T(8,128)(2,1)} copy(bf16[512,5120]{1,0:T(8,128)(2,1)} %get-tuple-element.46) | data formatting | bytes 10485760 | tf_op jit(solution)/shard_map/cond | solution.py:37
  46.2 7.9 %copy.34 = bf16[512,5120]{1,0:T(8,128)(2,1)} copy(bf16[512,5120]{0,1:T(8,128)(2,1)} %copy.25) | data formatting | bytes 10485760
  54.1 1.3 copy-done
  55.4 0.8 copy.23
  56.2 66.3 %reduce-scatter.16.cloned.1.call-done = bf16[128,5120]{1,0:T(8,128)(2,1)} async-done(((bf16[512,5120]{1,0:T(8,128)(2,1)}), bf16[128,5120]{1,0:T(8,128)(2,1)}) %reduce-scatter.16.cloned.1.call-update) | async-done | bytes 1310736
  122.5 1.8 copy.35
  124.2 0.3 add_convert_fusion.3
  124.6 1.3 collective-permute-start
  125.9 30.2 %collective-permute-done = bf16[128,5120]{0,1:T(8,128)(2,1)S(1)} collective-permute-done((bf16[128,5120]{0,1:T(8,128)(2,1)S(1)}, bf16[128,5120]{0,1:T(8,128)(2,1)S(1)}, u32[]{:S(2)}, u32[]{:S(2)}) %collective-permute-start) | collective-permute-done | bytes 1310752 | tf_op jit(solution)/shard_map/ppermute | solution.py:10
  156.1 1.4 copy.26
  157.6 5.1 all-to-all-start.1
  162.6 17.9 %all-to-all-done.1 = bf16[128,4,1280]{2,0,1:T(8,128)(2,1)S(1)} async-done(((bf16[128,4,1280]{2,0,1:T(8,128)(2,1)}), bf16[128,4,1280]{2,0,1:T(8,128)(2,1)S(1)}, u32[]{:S(2)}, u32[]{:S(2)}) %all-to-all-start.1) | async-done | bytes 1310752 | tf_op jit(solution)/shard_map/all_to_all | solution.py:26
  180.5 1.1 copy-done.6
  181.6 3.0 conditional.5
  181.6 3.0 broadcast.9
  184.6 7.9 %copy.27 = bf16[512,5120]{0,1:T(8,128)(2,1)} copy(bf16[512,5120]{1,0:T(8,128)(2,1)} %get-tuple-element.47) | data formatting | bytes 10485760 | tf_op jit(solution)/shard_map/cond | solution.py:37
  192.6 7.9 %copy.36 = bf16[512,5120]{1,0:T(8,128)(2,1)} copy(bf16[512,5120]{0,1:T(8,128)(2,1)} %copy.27) | data formatting | bytes 10485760
  200.4 68.0 %reduce-scatter.18.cloned.1.call-done = bf16[128,5120]{1,0:T(8,128)(2,1)} async-done(((bf16[512,5120]{1,0:T(8,128)(2,1)}), bf16[128,5120]{1,0:T(8,128)(2,1)}) %reduce-scatter.18.cloned.1.call-update) | async-done | bytes 1310736
  268.4 1.8 copy.37
  270.2 0.3 add_convert_fusion.2
  270.6 1.3 collective-permute-start.1
  271.9 30.2 %collective-permute-done.1 = bf16[128,5120]{0,1:T(8,128)(2,1)S(1)} collective-permute-done((bf16[128,5120]{0,1:T(8,128)(2,1)S(1)}, bf16[128,5120]{0,1:T(8,128)(2,1)S(1)}, u32[]{:S(2)}, u32[]{:S(2)}) %collective-permute-start.1) | collective-permute-done | bytes 1310752 | tf_op jit(solution)/shard_map/ppermute | solution.py:10
  302.1 1.4 copy.28
  303.5 5.1 all-to-all-start.2
  308.6 17.9 %all-to-all-done.2 = bf16[128,4,1280]{2,0,1:T(8,128)(2,1)S(1)} async-done(((bf16[128,4,1280]{2,0,1:T(8,128)(2,1)}), bf16[128,4,1280]{2,0,1:T(8,128)(2,1)S(1)}, u32[]{:S(2)}, u32[]{:S(2)}) %all-to-all-start.2) | async-done | bytes 1310752 | tf_op jit(solution)/shard_map/all_to_all | solution.py:26
  326.5 1.1 copy-done.7
  327.6 3.0 conditional.6
  327.6 3.0 broadcast.10
  330.6 7.9 %copy.29 = bf16[512,5120]{0,1:T(8,128)(2,1)} copy(bf16[512,5120]{1,0:T(8,128)(2,1)} %get-tuple-element.48) | data formatting | bytes 10485760 | tf_op jit(solution)/shard_map/cond | solution.py:37
  338.5 7.9 %copy.38 = bf16[512,5120]{1,0:T(8,128)(2,1)} copy(bf16[512,5120]{0,1:T(8,128)(2,1)} %copy.29) | data formatting | bytes 10485760
  346.4 0.0 all-gather.3.cloned.1.call-start
  346.5 0.5 all-gather.3.cloned.1.call-update
  347.0 65.9 %reduce-scatter.20.cloned.1.call-done = bf16[128,5120]{1,0:T(8,128)(2,1)} async-done(((bf16[512,5120]{1,0:T(8,128)(2,1)}), bf16[128,5120]{1,0:T(8,128)(2,1)}) %reduce-scatter.20.cloned.1.call-update) | async-done | bytes 1310736
  412.9 1.8 copy.39
  414.7 0.3 add_convert_fusion.1
  415.1 1.3 collective-permute-start.2
  416.4 30.3 %collective-permute-done.2 = bf16[128,5120]{0,1:T(8,128)(2,1)S(1)} collective-permute-done((bf16[128,5120]{0,1:T(8,128)(2,1)S(1)}, bf16[128,5120]{0,1:T(8,128)(2,1)S(1)}, u32[]{:S(2)}, u32[]{:S(2)}) %collective-permute-start.2) | collective-permute-done | bytes 1310752 | tf_op jit(solution)/shard_map/ppermute | solution.py:10
  446.7 1.4 copy.30
  448.1 5.0 all-to-all-start.3
  453.1 17.9 %all-to-all-done.3 = bf16[128,4,1280]{2,0,1:T(8,128)(2,1)S(1)} async-done(((bf16[128,4,1280]{2,0,1:T(8,128)(2,1)}), bf16[128,4,1280]{2,0,1:T(8,128)(2,1)S(1)}, u32[]{:S(2)}, u32[]{:S(2)}) %all-to-all-start.3) | async-done | bytes 1310752 | tf_op jit(solution)/shard_map/all_to_all | solution.py:26
  471.0 1.1 copy-done.8
  472.1 13.4 %conditional.7 = (bf16[512,5120]{1,0:T(8,128)(2,1)}) conditional(s32[]{:T(128)} %convert_element_type.83, () %tuple.38, (bf16[512,1280]{1,0:T(8,128)(2,1)S(1)}, bf16[5120,1280]{1,0:T(8,128)(2,1)}) %tuple.72), branch_computations={%region_9.10_spmd, %region_10.11_spmd} | conditional | flops 6710886400 | bytes 19660808 | solution.py:37
  472.1 13.4 %fusion.17 = bf16[512,5120]{1,0:T(8,128)(2,1)} fusion(bf16[512,1280]{1,0:T(8,128)(2,1)S(1)} %get-tuple-element.34, bf16[5120,1280]{1,0:T(8,128)(2,1)} %get-tuple-element.35), kind=kOutput, calls=%fused_computation.24 | convolution fusion | flops 6710886400 | bytes 19660800 | tf_op jit(solution)/shard_map/cond/branch_1_fun/dot_general | solution.py:29
  485.5 8.0 %copy.31 = bf16[512,5120]{0,1:T(8,128)(2,1)} copy(bf16[512,5120]{1,0:T(8,128)(2,1)} %get-tuple-element.49) | data formatting | bytes 10485760 | tf_op jit(solution)/shard_map/cond | solution.py:37
  493.4 8.0 %copy.40 = bf16[512,5120]{1,0:T(8,128)(2,1)} copy(bf16[512,5120]{0,1:T(8,128)(2,1)} %copy.31) | data formatting | bytes 10485760
  501.4 0.3 reduce-scatter.24.cloned.1.call-start
  501.7 0.0 all-gather.3.cloned.1.call-done
  501.7 1.0 copy-done.5
  502.7 12.3 %fusion = bf16[5120,1280]{0,1:T(8,128)(2,1)} fusion(bf16[1,512,5120]{2,1,0:T(8,128)(2,1)} %all-gather.3.cloned.1.call-done, bf16[512,1280]{1,0:T(8,128)(2,1)} %bitcast.54, bf16[512,1280]{1,0:T(8,128)(2,1)} %bitcast.52, bf16[512,1280]{1,0:T(8,128)(2,1)} %bitcast.50, bf16[512,1280]{1,0:T(8,128)(2,1)S(1)} %bitcast.48, pred[]{:T(512)S(6)} %eq.13, pred[]{:T(512)S(6)} %eq.14, ...), kind=kOutput, calls=%fused_computation.1 | convolution fusion | flops 6720061440 | bytes 23592964 | tf_op jit(solution)/shard_map/dot_general | solution.py:49
  515.0 17.9 %copy.42 = bf16[5120,1280]{1,0:T(8,128)(2,1)} copy(bf16[5120,1280]{0,1:T(8,128)(2,1)} %fusion) | data formatting | bytes 26214400
  532.9 23.7 %reduce-scatter.22.cloned.1.call-done = bf16[128,5120]{1,0:T(8,128)(2,1)} async-done(((bf16[512,5120]{1,0:T(8,128)(2,1)}), bf16[128,5120]{1,0:T(8,128)(2,1)}) %reduce-scatter.22.cloned.1.call-update) | async-done | bytes 1310736
  556.6 1.8 copy.41
  558.4 1.6 fusion.3
  559.9 2.4 copy.32
  562.4 133.1 %reduce-scatter.24.cloned.1.call-done = bf16[640,1280]{1,0:T(8,128)(2,1)} async-done(((bf16[5120,1280]{1,0:T(8,128)(2,1)}), bf16[640,1280]{1,0:T(8,128)(2,1)}) %reduce-scatter.24.cloned.1.call-update) | async-done | bytes 1638416
  695.5 3.5 copy.43
  699.0 1.6 bitcast_convert_fusion
  700.6 3.0 copy.33
  (21 shorter events, 0.1 us)
Async XLA Ops:
  9.6 24.6 %all-to-all-start = ((bf16[128,4,1280]{2,0,1:T(8,128)(2,1)}), bf16[128,4,1280]{2,0,1:T(8,128)(2,1)S(1)}, u32[]{:S(2)}, u32[]{:S(2)}) async-start(bf16[128,4,1280]{2,0,1:T(8,128)(2,1)} %bitcast.42), calls=%async_computation | async-start | bytes 2621440 | tf_op jit(solution)/shard_map/all_to_all | solution.py:26
  16.3 106.2 %reduce-scatter.16.cloned.1.call-start = ((), (), s32[]{:S(2)}) async-start(), calls=%async_computation.10 | async-start | bytes 6553600
  34.2 1.1 copy-start.4
  54.1 1.3 copy-start
  124.6 31.5 %copy-start.1 = (bf16[128,5120]{0,1:T(8,128)(2,1)}, bf16[128,5120]{0,1:T(8,128)(2,1)S(1)}, u32[]{:S(2)}) copy-start(bf16[128,5120]{0,1:T(8,128)(2,1)S(1)} %add_convert_fusion.3) | copy-start | bytes 3932164
  124.6 31.5 %collective-permute-start = (bf16[128,5120]{0,1:T(8,128)(2,1)S(1)}, bf16[128,5120]{0,1:T(8,128)(2,1)S(1)}, u32[]{:S(2)}, u32[]{:S(2)}) collective-permute-start(bf16[128,5120]{0,1:T(8,128)(2,1)S(1)} %add_convert_fusion.3), channel_id=1, source_target_pairs={{32,0},{64,32},{96,64},{33,1},{65,33},{97,65},{34,2},{66,34},{98,6... | collective-permute-start | bytes 3932168 | tf_op jit(solution)/shard_map/ppermute | solution.py:10
  157.6 23.0 %all-to-all-start.1 = ((bf16[128,4,1280]{2,0,1:T(8,128)(2,1)}), bf16[128,4,1280]{2,0,1:T(8,128)(2,1)S(1)}, u32[]{:S(2)}, u32[]{:S(2)}) async-start(bf16[128,4,1280]{2,0,1:T(8,128)(2,1)} %copy.26), calls=%async_computation.1 | async-start | bytes 2621440 | tf_op jit(solution)/shard_map/all_to_all | solution.py:26
  162.6 105.8 %reduce-scatter.18.cloned.1.call-start = ((), (), s32[]{:S(2)}) async-start(), calls=%async_computation.11 | async-start | bytes 6553600
  180.5 1.1 copy-start.6
  270.6 31.6 %copy-start.2 = (bf16[128,5120]{0,1:T(8,128)(2,1)}, bf16[128,5120]{0,1:T(8,128)(2,1)S(1)}, u32[]{:S(2)}) copy-start(bf16[128,5120]{0,1:T(8,128)(2,1)S(1)} %add_convert_fusion.2) | copy-start | bytes 3932164
  270.6 31.5 %collective-permute-start.1 = (bf16[128,5120]{0,1:T(8,128)(2,1)S(1)}, bf16[128,5120]{0,1:T(8,128)(2,1)S(1)}, u32[]{:S(2)}, u32[]{:S(2)}) collective-permute-start(bf16[128,5120]{0,1:T(8,128)(2,1)S(1)} %add_convert_fusion.2), channel_id=1, source_target_pairs={{32,0},{64,32},{96,64},{33,1},{65,33},{97,65},{34,2},{66,34},{98,6... | collective-permute-start | bytes 3932168 | tf_op jit(solution)/shard_map/ppermute | solution.py:10
  303.5 23.0 %all-to-all-start.2 = ((bf16[128,4,1280]{2,0,1:T(8,128)(2,1)}), bf16[128,4,1280]{2,0,1:T(8,128)(2,1)S(1)}, u32[]{:S(2)}, u32[]{:S(2)}) async-start(bf16[128,4,1280]{2,0,1:T(8,128)(2,1)} %copy.28), calls=%async_computation.2 | async-start | bytes 2621440 | tf_op jit(solution)/shard_map/all_to_all | solution.py:26
  308.6 104.3 %reduce-scatter.20.cloned.1.call-start = ((), (), s32[]{:S(2)}) async-start(), calls=%async_computation.12 | async-start | bytes 6553600
  326.5 1.1 copy-start.7
  346.4 155.3 %all-gather.3.cloned.1.call-start = ((), (), s32[]{:S(2)}) async-start(), calls=%async_computation.9 | async-start | bytes 6553600 | tf_op jit(solution)/shard_map/all_gather | solution.py:47
  415.1 31.7 %copy-start.3 = (bf16[128,5120]{0,1:T(8,128)(2,1)}, bf16[128,5120]{0,1:T(8,128)(2,1)S(1)}, u32[]{:S(2)}) copy-start(bf16[128,5120]{0,1:T(8,128)(2,1)S(1)} %add_convert_fusion.1) | copy-start | bytes 3932164
  415.1 31.6 %collective-permute-start.2 = (bf16[128,5120]{0,1:T(8,128)(2,1)S(1)}, bf16[128,5120]{0,1:T(8,128)(2,1)S(1)}, u32[]{:S(2)}, u32[]{:S(2)}) collective-permute-start(bf16[128,5120]{0,1:T(8,128)(2,1)S(1)} %add_convert_fusion.1), channel_id=1, source_target_pairs={{32,0},{64,32},{96,64},{33,1},{65,33},{97,65},{34,2},{66,34},{98,6... | collective-permute-start | bytes 3932168 | tf_op jit(solution)/shard_map/ppermute | solution.py:10
  448.1 22.9 %all-to-all-start.3 = ((bf16[128,4,1280]{2,0,1:T(8,128)(2,1)}), bf16[128,4,1280]{2,0,1:T(8,128)(2,1)S(1)}, u32[]{:S(2)}, u32[]{:S(2)}) async-start(bf16[128,4,1280]{2,0,1:T(8,128)(2,1)} %copy.30), calls=%async_computation.3 | async-start | bytes 2621440 | tf_op jit(solution)/shard_map/all_to_all | solution.py:26
  453.1 103.5 %reduce-scatter.22.cloned.1.call-start = ((), (), s32[]{:S(2)}) async-start(), calls=%async_computation.13 | async-start | bytes 6553600
  471.0 1.1 copy-start.8
  501.4 1.3 copy-start.5
  501.4 194.1 %reduce-scatter.24.cloned.1.call-start = ((), (), s32[]{:S(2)}) async-start(), calls=%async_computation.14 | async-start | bytes 14745600
Sparse Core Ops, SparseCore 0:
  54.2 68.1 reduce-scatter.15
  200.6 67.8 reduce-scatter.17
  346.5 66.3 reduce-scatter.19
  414.6 44.2 all-gather.2
  501.5 55.0 reduce-scatter.21
  558.9 136.5 reduce-scatter.23
where the time goes:
time: 713 us; the launch traced here: 710 us
  waiting for transfers between devices  520 us (73%)
  local copies, waits for them, and re-layouts  120 us (17%)
  starting transfers between devices  25.9 us (4%)
  matrix products  25.7 us (4%)
  between operations  14.2 us (2%)
    unnamed x11, waiting for transfers between devices  358 us
    ppermute x3, waiting for transfers between devices, from_behind(): return lax.ppermute(block, axis, route)  90.8 us
    unnamed x31, local copies, waits for them, and re-layouts  72.7 us
    all_to_all x4, waiting for transfers between devices, on_device(): lax.all_to_all(gradient, 'tensor', split_axis=1, concat_axis=0, tiled=True)  71.6 us
    cond x4, local copies, waits for them, and re-layouts, on_device(): lax.cond(on_duty, compute, nothing, columns).astype(jnp.bfloat16)  31.8 us
    all_to_all x4, starting transfers between devices, on_device(): lax.all_to_all(gradient, 'tensor', split_axis=1, concat_axis=0, tiled=True)  21.7 us
  transfers between devices with their start and end apart: 13, of which 12 were waited for; matrix products, arithmetic and copies ran while one was open for 10% of the time, Pallas kernels for 0%

commit v1 on v0

--- a/solution.py
+++ b/solution.py
@@ -23,7 +23,12 @@
     for rounds in range(sections):
         active = sections - 1 - rounds
         on_duty = section_index == active
-        columns = lax.all_to_all(gradient, "tensor", split_axis=1, concat_axis=0, tiled=True)
+        columns = jnp.concatenate(
+            lax.all_to_all(
+                jnp.stack(jnp.split(gradient, lax.axis_size("tensor"), axis=1)), "tensor", 0, 0
+            ),
+            axis=0,
+        )
 
         def compute(operand):
             return lax.dot_general(

time: 713 us -> 646 us (0.906)
  local copies, waits for them, and re-layouts: 120 us -> 35.9 us
  other arithmetic: 4.22 us -> 14.2 us
    reduce_scatter x0 -> x4, waiting for transfers between devices: none -> 228 us  [on_device(): lax.psum_scatter(lax.cond(on_duty, compute, nothing, columns).astype(jnp....]
    unnamed x11 -> x7, waiting for transfers between devices: 358 us -> 136 us
    unnamed x31 -> x11, local copies, waits for them, and re-layouts: 72.7 us -> 25.4 us
    cond x4 -> x0, local copies, waits for them, and re-layouts: 31.8 us -> none  [on_device(): lax.cond(on_duty, compute, nothing, columns).astype(jnp.bfloat16)]
  transfers between devices with their start and end apart: 13 -> 13, of which waited for: 12 -> 12; matrix products, arithmetic and copies ran while one was open for 10% -> 8% of each run, Pallas kernels for 0% -> 0%
where the time goes in v1:
time: 646 us; the launch traced here: 645 us
  waiting for transfers between devices  527 us (82%)
  local copies, waits for them, and re-layouts  35.9 us (6%)
  starting transfers between devices  28.1 us (4%)
  matrix products  26 us (4%)
  other arithmetic  14.2 us (2%)
  between operations  14.2 us (2%)
    reduce_scatter x4, waiting for transfers between devices, on_device(): lax.psum_scatter(lax.cond(on_duty, compute, nothing, columns).astype(jnp....  228 us
    unnamed x7, waiting for transfers between devices  136 us
    ppermute x3, waiting for transfers between devices, from_behind(): return lax.ppermute(block, axis, route)  90.8 us
    all_to_all x4, waiting for transfers between devices, on_device(): lax.all_to_all(jnp.stack(jnp.split(gradient, lax.axis_size('tensor'), axi...  71.9 us
    unnamed x11, local copies, waits for them, and re-layouts  25.4 us
    all_to_all x4, starting transfers between devices, on_device(): lax.all_to_all(jnp.stack(jnp.split(gradient, lax.axis_size('tensor'), axi...  23.9 us
    dot_general x1, matrix products, compute(): lax.dot_general(operand, weight_cols, (((1,), (1,)), ((), ())), preferred...  13.6 us
  transfers between devices with their start and end apart: 13, of which 12 were waited for; matrix products, arithmetic and copies ran while one was open for 8% of the time, Pallas kernels for 0%

profile of v1, /device:TPU:1, one launch (start us, length us, event | category | flops | bytes accessed | tf_op | source)
XLA Modules:
  0.0 645.3 jit_solution(10064587181311850208)
XLA Ops:
  7.2 1.4 slice_bitcast_fusion.15
  8.5 1.2 pad_maximum_fusion
  9.8 6.6 %all-to-all-start = ((bf16[4,128,1280]{2,1,0:T(8,128)(2,1)}), bf16[4,128,1280]{2,1,0:T(8,128)(2,1)S(1)}, u32[]{:S(2)}, u32[]{:S(2)}) async-start(bf16[4,128,1280]{2,1,0:T(8,128)(2,1)} %pad_maximum_fusion), calls=%async_computation | async-start | bytes 2621440 | tf_op jit(solution)/shard_map/all_to_all | solution.py:27
  16.4 0.0 reduce-scatter.8.cloned.1.call-start
  16.4 17.9 %all-to-all-done = bf16[4,128,1280]{2,1,0:T(8,128)(2,1)S(1)} async-done(((bf16[4,128,1280]{2,1,0:T(8,128)(2,1)}), bf16[4,128,1280]{2,1,0:T(8,128)(2,1)S(1)}, u32[]{:S(2)}, u32[]{:S(2)}) %all-to-all-start) | async-done | bytes 1310752 | tf_op jit(solution)/shard_map/all_to_all | solution.py:27
  34.3 0.0 copy-start.3
  34.3 1.1 copy-done.3
  35.4 3.0 conditional.4
  35.4 3.0 broadcast.8
  38.3 0.0 reduce-scatter.8.cloned.1.call-update
  38.4 68.4 %reduce-scatter.8.cloned.1.call-done = bf16[128,5120]{1,0:T(8,128)(2,1)} async-done(((bf16[512,5120]{1,0:T(8,128)(2,1)}), bf16[128,5120]{1,0:T(8,128)(2,1)}) %reduce-scatter.8.cloned.1.call-update) | async-done | bytes 1310736 | tf_op jit(solution)/shard_map/reduce_scatter | solution.py:41
  106.8 0.0 copy-done
  106.8 1.6 add_convert_fusion.3
  108.4 1.3 collective-permute-start
  109.7 30.3 %collective-permute-done = bf16[128,5120]{1,0:T(8,128)(2,1)S(1)} collective-permute-done((bf16[128,5120]{1,0:T(8,128)(2,1)S(1)}, bf16[128,5120]{1,0:T(8,128)(2,1)S(1)}, u32[]{:S(2)}, u32[]{:S(2)}) %collective-permute-start) | collective-permute-done | bytes 1310752 | tf_op jit(solution)/shard_map/ppermute | solution.py:10
  140.0 0.1 slice_bitcast_fusion.11
  140.0 1.2 pad_maximum_fusion.1
  141.3 5.8 all-to-all-start.1
  147.0 0.0 reduce-scatter.10.cloned.1.call-start
  147.0 18.0 %all-to-all-done.1 = bf16[4,128,1280]{2,1,0:T(8,128)(2,1)} async-done(((bf16[4,128,1280]{2,1,0:T(8,128)(2,1)}), bf16[4,128,1280]{2,1,0:T(8,128)(2,1)}, u32[]{:S(2)}, u32[]{:S(2)}) %all-to-all-start.1) | async-done | bytes 1310752 | tf_op jit(solution)/shard_map/all_to_all | solution.py:27
  165.1 3.0 conditional.5
  165.1 3.0 broadcast.9
  168.0 0.0 reduce-scatter.10.cloned.1.call-update
  168.0 68.2 %reduce-scatter.10.cloned.1.call-done = bf16[128,5120]{1,0:T(8,128)(2,1)} async-done(((bf16[512,5120]{1,0:T(8,128)(2,1)}), bf16[128,5120]{1,0:T(8,128)(2,1)}) %reduce-scatter.10.cloned.1.call-update) | async-done | bytes 1310736 | tf_op jit(solution)/shard_map/reduce_scatter | solution.py:41
  236.3 1.6 add_convert_fusion.2
  237.9 0.0 copy-start.1
  237.9 1.3 collective-permute-start.1
  239.2 30.2 %collective-permute-done.1 = bf16[128,5120]{1,0:T(8,128)(2,1)S(1)} collective-permute-done((bf16[128,5120]{1,0:T(8,128)(2,1)S(1)}, bf16[128,5120]{1,0:T(8,128)(2,1)S(1)}, u32[]{:S(2)}, u32[]{:S(2)}) %collective-permute-start.1) | collective-permute-done | bytes 1310752 | tf_op jit(solution)/shard_map/ppermute | solution.py:10
  269.5 0.1 slice_bitcast_fusion.7
  269.5 0.0 copy-done.1
  269.6 1.2 pad_maximum_fusion.2
  270.8 5.8 all-to-all-start.2
  276.6 0.0 reduce-scatter.12.cloned.1.call-start
  276.6 18.0 %all-to-all-done.2 = bf16[4,128,1280]{2,1,0:T(8,128)(2,1)} async-done(((bf16[4,128,1280]{2,1,0:T(8,128)(2,1)}), bf16[4,128,1280]{2,1,0:T(8,128)(2,1)}, u32[]{:S(2)}, u32[]{:S(2)}) %all-to-all-start.2) | async-done | bytes 1310752 | tf_op jit(solution)/shard_map/all_to_all | solution.py:27
  294.6 3.0 conditional.6
  294.6 3.0 broadcast.10
  297.6 0.0 reduce-scatter.12.cloned.1.call-update
  297.6 0.2 all-gather.3.cloned.1.call-start
  297.8 0.3 all-gather.3.cloned.1.call-update
  298.2 66.2 %reduce-scatter.12.cloned.1.call-done = bf16[128,5120]{1,0:T(8,128)(2,1)} async-done(((bf16[512,5120]{1,0:T(8,128)(2,1)}), bf16[128,5120]{1,0:T(8,128)(2,1)}) %reduce-scatter.12.cloned.1.call-update) | async-done | bytes 1310736 | tf_op jit(solution)/shard_map/reduce_scatter | solution.py:41
  364.4 1.6 add_convert_fusion.1
  366.0 0.0 copy-start.2
  366.0 1.3 collective-permute-start.2
  367.3 30.3 %collective-permute-done.2 = bf16[128,5120]{1,0:T(8,128)(2,1)S(1)} collective-permute-done((bf16[128,5120]{1,0:T(8,128)(2,1)S(1)}, bf16[128,5120]{1,0:T(8,128)(2,1)S(1)}, u32[]{:S(2)}, u32[]{:S(2)}) %collective-permute-start.2) | collective-permute-done | bytes 1310752 | tf_op jit(solution)/shard_map/ppermute | solution.py:10
  397.6 0.1 slice_bitcast_fusion.3
  397.7 0.0 copy-done.2
  397.7 1.2 pad_maximum_fusion.3
  399.0 5.7 all-to-all-start.3
  404.7 0.0 reduce-scatter.14.cloned.1.call-start
  404.7 18.0 %all-to-all-done.3 = bf16[4,128,1280]{2,1,0:T(8,128)(2,1)} async-done(((bf16[4,128,1280]{2,1,0:T(8,128)(2,1)}), bf16[4,128,1280]{2,1,0:T(8,128)(2,1)}, u32[]{:S(2)}, u32[]{:S(2)}) %all-to-all-start.3) | async-done | bytes 1310752 | tf_op jit(solution)/shard_map/all_to_all | solution.py:27
  422.7 13.6 %conditional.7 = (bf16[512,5120]{1,0:T(8,128)(2,1)}) conditional(s32[]{:T(128)} %convert_element_type.83, () %tuple.38, (bf16[512,1280]{1,0:T(8,128)(2,1)}, bf16[5120,1280]{1,0:T(8,128)(2,1)}) %tuple.79), branch_computations={%region_9.10_spmd, %region_10.11_spmd} | conditional | flops 6710886400 | bytes 19660808 | solution.py:42
  422.7 13.6 %fusion.17 = bf16[512,5120]{1,0:T(8,128)(2,1)} fusion(bf16[512,1280]{1,0:T(8,128)(2,1)} %get-tuple-element.34, bf16[5120,1280]{1,0:T(8,128)(2,1)} %get-tuple-element.35), kind=kOutput, calls=%fused_computation.43 | convolution fusion | flops 6710886400 | bytes 19660800 | tf_op jit(solution)/shard_map/cond/branch_1_fun/dot_general | solution.py:34
  436.3 0.0 reduce-scatter.14.cloned.1.call-update
  436.3 0.0 reduce-scatter.16.cloned.1.call-start
  436.4 0.0 all-gather.3.cloned.1.call-done
  436.4 12.4 %fusion = bf16[5120,1280]{0,1:T(8,128)(2,1)} fusion(bf16[1,512,5120]{2,1,0:T(8,128)(2,1)} %all-gather.3.cloned.1.call-done, bf16[512,1280]{1,0:T(8,128)(2,1)} %bitcast.20, bf16[512,1280]{1,0:T(8,128)(2,1)} %bitcast.15, bf16[512,1280]{1,0:T(8,128)(2,1)} %bitcast.10, bf16[512,1280]{1,0:T(8,128)(2,1)} %bitcast.57, pred[]{:T(512)S(6)} %eq.13, pred[]{:T(512)S(6)} %eq.14, ...), kind=kOutput, calls=%fused_computation.1 | convolution fusion | flops 6720061440 | bytes 23592964 | tf_op jit(solution)/shard_map/dot_general | solution.py:54
  448.8 17.8 %copy.7 = bf16[5120,1280]{1,0:T(8,128)(2,1)} copy(bf16[5120,1280]{0,1:T(8,128)(2,1)} %fusion) | data formatting | bytes 26214400
  466.6 0.0 reduce-scatter.16.cloned.1.call-update
  466.6 24.8 %reduce-scatter.14.cloned.1.call-done = bf16[128,5120]{1,0:T(8,128)(2,1)} async-done(((bf16[512,5120]{1,0:T(8,128)(2,1)}), bf16[128,5120]{1,0:T(8,128)(2,1)}) %reduce-scatter.14.cloned.1.call-update) | async-done | bytes 1310736 | tf_op jit(solution)/shard_map/reduce_scatter | solution.py:41
  491.4 2.8 fusion.3
  494.3 136.0 %reduce-scatter.16.cloned.1.call-done = bf16[640,1280]{1,0:T(8,128)(2,1)} async-done(((bf16[5120,1280]{1,0:T(8,128)(2,1)}), bf16[640,1280]{1,0:T(8,128)(2,1)}) %reduce-scatter.16.cloned.1.call-update) | async-done | bytes 1638416
  630.3 3.5 copy.8
  633.8 1.6 bitcast_convert_fusion
  635.5 3.0 copy.6
  (1 shorter events, 0.0 us)
Async XLA Ops:
  9.8 24.6 %all-to-all-start = ((bf16[4,128,1280]{2,1,0:T(8,128)(2,1)}), bf16[4,128,1280]{2,1,0:T(8,128)(2,1)S(1)}, u32[]{:S(2)}, u32[]{:S(2)}) async-start(bf16[4,128,1280]{2,1,0:T(8,128)(2,1)} %pad_maximum_fusion), calls=%async_computation | async-start | bytes 2621440 | tf_op jit(solution)/shard_map/all_to_all | solution.py:27
  16.4 90.4 %reduce-scatter.8.cloned.1.call-start = ((), (), s32[]{:S(2)}) async-start(), calls=%async_computation.9 | async-start | bytes 6553600 | tf_op jit(solution)/shard_map/reduce_scatter | solution.py:41
  34.3 1.1 copy-start.3
  38.3 68.4 %copy-start = (bf16[128,5120]{1,0:T(8,128)(2,1)S(1)}, bf16[128,5120]{1,0:T(8,128)(2,1)}, u32[]{:S(2)}) copy-start(bf16[128,5120]{1,0:T(8,128)(2,1)} %param.13) | copy-start | bytes 3932164
  108.4 31.6 %collective-permute-start = (bf16[128,5120]{1,0:T(8,128)(2,1)S(1)}, bf16[128,5120]{1,0:T(8,128)(2,1)S(1)}, u32[]{:S(2)}, u32[]{:S(2)}) collective-permute-start(bf16[128,5120]{1,0:T(8,128)(2,1)S(1)} %add_convert_fusion.3), channel_id=1, source_target_pairs={{32,0},{64,32},{96,64},{33,1},{65,33},{97,65},{34,2},{66,34},{98,6... | collective-permute-start | bytes 3932168 | tf_op jit(solution)/shard_map/ppermute | solution.py:10
  141.3 23.8 %all-to-all-start.1 = ((bf16[4,128,1280]{2,1,0:T(8,128)(2,1)}), bf16[4,128,1280]{2,1,0:T(8,128)(2,1)}, u32[]{:S(2)}, u32[]{:S(2)}) async-start(bf16[4,128,1280]{2,1,0:T(8,128)(2,1)} %pad_maximum_fusion.1), calls=%async_computation.2 | async-start | bytes 2621440 | tf_op jit(solution)/shard_map/all_to_all | solution.py:27
  147.0 89.2 %reduce-scatter.10.cloned.1.call-start = ((), (), s32[]{:S(2)}) async-start(), calls=%async_computation.10 | async-start | bytes 6553600 | tf_op jit(solution)/shard_map/reduce_scatter | solution.py:41
  237.9 31.6 %copy-start.1 = (bf16[128,5120]{1,0:T(8,128)(2,1)}, bf16[128,5120]{1,0:T(8,128)(2,1)S(1)}, u32[]{:S(2)}) copy-start(bf16[128,5120]{1,0:T(8,128)(2,1)S(1)} %add_convert_fusion.2) | copy-start | bytes 3932164
  237.9 31.5 %collective-permute-start.1 = (bf16[128,5120]{1,0:T(8,128)(2,1)S(1)}, bf16[128,5120]{1,0:T(8,128)(2,1)S(1)}, u32[]{:S(2)}, u32[]{:S(2)}) collective-permute-start(bf16[128,5120]{1,0:T(8,128)(2,1)S(1)} %add_convert_fusion.2), channel_id=1, source_target_pairs={{32,0},{64,32},{96,64},{33,1},{65,33},{97,65},{34,2},{66,34},{98,6... | collective-permute-start | bytes 3932168 | tf_op jit(solution)/shard_map/ppermute | solution.py:10
  270.8 23.8 %all-to-all-start.2 = ((bf16[4,128,1280]{2,1,0:T(8,128)(2,1)}), bf16[4,128,1280]{2,1,0:T(8,128)(2,1)}, u32[]{:S(2)}, u32[]{:S(2)}) async-start(bf16[4,128,1280]{2,1,0:T(8,128)(2,1)} %pad_maximum_fusion.2), calls=%async_computation.4 | async-start | bytes 2621440 | tf_op jit(solution)/shard_map/all_to_all | solution.py:27
  276.6 87.8 %reduce-scatter.12.cloned.1.call-start = ((), (), s32[]{:S(2)}) async-start(), calls=%async_computation.11 | async-start | bytes 6553600 | tf_op jit(solution)/shard_map/reduce_scatter | solution.py:41
  297.6 138.8 %all-gather.3.cloned.1.call-start = ((), (), s32[]{:S(2)}) async-start(), calls=%async_computation.13 | async-start | bytes 6553600 | tf_op jit(solution)/shard_map/all_gather | solution.py:52
  366.0 31.7 %copy-start.2 = (bf16[128,5120]{1,0:T(8,128)(2,1)}, bf16[128,5120]{1,0:T(8,128)(2,1)S(1)}, u32[]{:S(2)}) copy-start(bf16[128,5120]{1,0:T(8,128)(2,1)S(1)} %add_convert_fusion.1) | copy-start | bytes 3932164
  366.0 31.6 %collective-permute-start.2 = (bf16[128,5120]{1,0:T(8,128)(2,1)S(1)}, bf16[128,5120]{1,0:T(8,128)(2,1)S(1)}, u32[]{:S(2)}, u32[]{:S(2)}) collective-permute-start(bf16[128,5120]{1,0:T(8,128)(2,1)S(1)} %add_convert_fusion.1), channel_id=1, source_target_pairs={{32,0},{64,32},{96,64},{33,1},{65,33},{97,65},{34,2},{66,34},{98,6... | collective-permute-start | bytes 3932168 | tf_op jit(solution)/shard_map/ppermute | solution.py:10
  399.0 23.7 %all-to-all-start.3 = ((bf16[4,128,1280]{2,1,0:T(8,128)(2,1)}), bf16[4,128,1280]{2,1,0:T(8,128)(2,1)}, u32[]{:S(2)}, u32[]{:S(2)}) async-start(bf16[4,128,1280]{2,1,0:T(8,128)(2,1)} %pad_maximum_fusion.3), calls=%async_computation.6 | async-start | bytes 2621440 | tf_op jit(solution)/shard_map/all_to_all | solution.py:27
  404.7 86.8 %reduce-scatter.14.cloned.1.call-start = ((), (), s32[]{:S(2)}) async-start(), calls=%async_computation.12 | async-start | bytes 6553600 | tf_op jit(solution)/shard_map/reduce_scatter | solution.py:41
  436.3 194.0 %reduce-scatter.16.cloned.1.call-start = ((), (), s32[]{:S(2)}) async-start(), calls=%async_computation.14 | async-start | bytes 14745600
Sparse Core Ops, SparseCore 0:
  38.5 68.2 reduce-scatter.7
  168.2 68.0 reduce-scatter.9
  297.7 66.6 reduce-scatter.11
  366.0 44.2 all-gather.2
  436.4 54.9 reduce-scatter.13
  493.7 136.5 reduce-scatter.15
